TPU v7x, 32 devices: a whole 2x2x4 slice. The times are simulated.
32 devices in a mesh: pipe: 2 (over core), tensor: 4 (over y, x), dp: 4 (over z).
Axes of the slice: x: 2, y: 2, z: 4, core: 2. Of those that a mesh axis runs over, the one named last changes fastest.
Arguments:
- layer_input: bfloat16 [2, 512, 768], P(None, 'dp'), may hold values from -6 to 6
- enc_states: bfloat16 [2, 1024, 768], P(None, 'dp'), may hold values from -6 to 6
- out_grad: bfloat16 [2, 512, 768], P(None, 'dp'), may hold values from -6 to 6
- dec_seg: int32 [2, 512], P(None, 'dp'), may hold values from 0 to 3, as said below
- enc_seg: int32 [2, 1024], P(None, 'dp'), may hold values from 0 to 3, as said below
- buckets: int32 [128], replicated, may hold values from 0 to 31, as said below
- sa_q: bfloat16 [2, 768, 768], P('pipe', 'dp', 'tensor'), may hold values from -0.02734375 to 0.02734375
- sa_k: bfloat16 [2, 768, 768], P('pipe', 'dp', 'tensor'), may hold values from -0.21875 to 0.21875
- sa_v: bfloat16 [2, 768, 768], P('pipe', 'dp', 'tensor'), may hold values from -0.21875 to 0.21875
- sa_o: bfloat16 [2, 768, 768], P('pipe', 'tensor', 'dp'), may hold values from -0.875 to 0.875
- ca_q: bfloat16 [2, 768, 768], P('pipe', 'dp', 'tensor'), may hold values from -0.02734375 to 0.02734375
- ca_k: bfloat16 [2, 768, 768], P('pipe', 'dp', 'tensor'), may hold values from -0.21875 to 0.21875
- ca_v: bfloat16 [2, 768, 768], P('pipe', 'dp', 'tensor'), may hold values from -0.21875 to 0.21875
- ca_o: bfloat16 [2, 768, 768], P('pipe', 'tensor', 'dp'), may hold values from -0.875 to 0.875
- ff_gate: bfloat16 [2, 768, 2048], P('pipe', 'dp', 'tensor'), may hold values from -0.21875 to 0.21875
- ff_up: bfloat16 [2, 768, 2048], P('pipe', 'dp', 'tensor'), may hold values from -0.21875 to 0.21875
- ff_down: bfloat16 [2, 2048, 768], P('pipe', 'tensor', 'dp'), may hold values from -0.125 to 0.125
- norm_gains: bfloat16 [2, 3, 768], P('pipe', None, 'dp'), may hold values from 0.5 to 1.5
- rel_table: bfloat16 [2, 32, 12], P('pipe', 'dp', 'tensor'), may hold values from -4 to 4
Outputs:
- section_out: bfloat16 [2, 2, 512, 768], P('pipe', None, 'dp')
- section_in_grad: float32 [2, 2, 512, 768], P('pipe', None, 'dp')
- enc_grad: float32 [2, 2, 1024, 768], P('pipe', None, 'dp', 'tensor')
- grad_sa_q: float32 [2, 768, 768], P('pipe', 'dp', 'tensor')
- grad_sa_k: float32 [2, 768, 768], P('pipe', 'dp', 'tensor')
- grad_sa_v: float32 [2, 768, 768], P('pipe', 'dp', 'tensor')
- grad_sa_o: float32 [2, 768, 768], P('pipe', 'tensor', 'dp')
- grad_ca_q: float32 [2, 768, 768], P('pipe', 'dp', 'tensor')
- grad_ca_k: float32 [2, 768, 768], P('pipe', 'dp', 'tensor')
- grad_ca_v: float32 [2, 768, 768], P('pipe', 'dp', 'tensor')
- grad_ca_o: float32 [2, 768, 768], P('pipe', 'tensor', 'dp')
- grad_ff_gate: float32 [2, 768, 2048], P('pipe', 'dp', 'tensor')
- grad_ff_up: float32 [2, 768, 2048], P('pipe', 'dp', 'tensor')
- grad_ff_down: float32 [2, 2048, 768], P('pipe', 'tensor', 'dp')
- grad_norm_gains: float32 [2, 3, 768], P('pipe', None, 'dp')
- grad_rel_table: float32 [2, 32, 12], P('pipe', 'dp', 'tensor')
Inputs may be any that keep to these rules, and one draw needn't show every extreme that they name: `dec_seg`: within each aligned block of 128 entries (one micro-batch of one group) the ids start at 0, never fall, and step up by one at exactly 3 positions. `enc_seg`: within each aligned block of 256 entries the ids start at 0, never fall, and step up by one at exactly 3 positions, so every decoder sequence has encoder tokens of its own id. `buckets`: Non-decreasing in the distance, 0 at distance 0, rising by at most one a step, and reaching 31.
All inputs are finite; a program needn't handle non-finite values.
Results may differ from a plain program's by a relative error of at most 0.033.
Values may be sent and summed in bfloat16 or wider, within the bound.
A program may use at most 128 MiB of HBM per device.

v0:
```python
import jax
import jax.numpy as jnp
from jax import lax
from jax.sharding import PartitionSpec as P

D = 768
HEAD = 64
BUCKETS = 32
MAXD = 128


EPS = 1e-06


def passed_along(value, axis, steps):
    count = lax.axis_size(axis)
    first, last = (max(0, -steps), min(count, count - steps))
    return lax.ppermute(value, axis, [(source, source + steps) for source in range(first, last)])


def product(form, left_side, right_side):
    return jnp.einsum(form, left_side, right_side, preferred_element_type=jnp.float32)


def rms_norm(values, gain):
    return values * lax.rsqrt(jnp.mean(values * values, axis=-1, keepdims=True) + EPS) * gain


def norm_back(values, gain, cotangent):
    _, pull_back = jax.vjp(rms_norm, values, gain)
    return pull_back(cotangent)


def gelu_tanh(values):
    return jax.nn.gelu(values, approximate=True)


def offset_spread(buckets, row_count):
    offsets = jnp.arange(2 * row_count - 1, dtype=jnp.int32)
    dist_of = jnp.clip(offsets - (row_count - 1), 0, MAXD - 1)
    bucket_of = jnp.sum(
        (dist_of[:, None] == jnp.arange(MAXD, dtype=jnp.int32)[None, :]).astype(jnp.int32)
        * buckets[None, :],
        axis=1,
    )
    return (bucket_of[:, None] == jnp.arange(BUCKETS, dtype=jnp.int32)[None, :]).astype(jnp.float32)


def bias_from_table(spread, table_float, row_count):
    offset_values = jnp.dot(spread, table_float, precision=lax.Precision.HIGHEST)
    reversed_rows = offset_values[::-1].T
    head_count = reversed_rows.shape[0]
    width = 4 * row_count - 3
    tiled = jnp.tile(reversed_rows, (1, 2 * row_count))[:, : row_count * width]
    return tiled.reshape(head_count, row_count, width)[:, :, row_count - 1 : 2 * row_count - 1]


def bias_grad(grad_scores, spread):
    head_count, row_count = (grad_scores.shape[0], grad_scores.shape[1])
    width = 4 * row_count - 3
    placed = jnp.pad(grad_scores, ((0, 0), (0, 0), (row_count - 1, width - 2 * row_count + 1)))
    flat = jnp.pad(placed.reshape(head_count, row_count * width), ((0, 0), (0, row_count)))
    folded = jnp.sum(flat.reshape(head_count, 2 * row_count, 2 * row_count - 1), axis=1)
    by_offset = folded[:, ::-1]
    return jnp.dot(spread.T, by_offset.T, precision=lax.Precision.HIGHEST)


def build_masks(dec_ids, enc_ids):
    row_count = dec_ids.shape[0]
    row_ids = jnp.arange(row_count, dtype=jnp.int32)
    allowed_self = (dec_ids[:, None] == dec_ids[None, :]) & (row_ids[None, :] <= row_ids[:, None])
    allowed_cross = dec_ids[:, None] == enc_ids[None, :]
    return (allowed_self, allowed_cross)


def local_terms(operands):
    running = None
    for left_side, right_side in operands:
        term = jnp.dot(left_side, right_side, preferred_element_type=jnp.float32)
        running = term if running is None else running + term
    return running


def forward_sum(operands):
    part_sum = lax.psum_scatter(local_terms(operands), "tensor", scatter_dimension=1, tiled=True)
    return lax.all_gather(part_sum, "tensor", axis=1, tiled=True)


def backward_sum(operands):
    part_sum = lax.psum_scatter(
        local_terms(operands).astype(jnp.bfloat16), "tensor", scatter_dimension=1, tiled=True
    ).astype(jnp.float32)
    return lax.all_gather(part_sum.astype(jnp.bfloat16), "tensor", axis=1, tiled=True).astype(
        part_sum.dtype
    )


def split_heads(values, head_count):
    return values.reshape(values.shape[0], head_count, values.shape[1] // head_count)


def attend(query, key_rows, value_rows, bias_block, allowed, head_count):
    query_heads = split_heads(query, head_count)
    key_heads = split_heads(key_rows, head_count)
    value_heads = split_heads(value_rows, head_count)
    scores = product("qhd,khd->hqk", query_heads, key_heads)
    if bias_block is not None:
        scores = scores + bias_block
    scores = jnp.where(allowed[None], scores, -1e30)
    log_total = jnp.log(jnp.sum(jnp.exp(scores), axis=-1, keepdims=True))
    probs = jnp.exp(scores - log_total).astype(jnp.bfloat16)
    attended = product("hqk,khd->qhd", probs, value_heads)
    return (attended.reshape(query.shape[0], query.shape[1]).astype(jnp.bfloat16), log_total)


def attend_back(
    grad_attended, query, key_rows, value_rows, bias_block, allowed, log_total, attended, head_count
):
    query_heads = split_heads(query, head_count)
    key_heads = split_heads(key_rows, head_count)
    value_heads = split_heads(value_rows, head_count)
    scores = product("qhd,khd->hqk", query_heads, key_heads)
    if bias_block is not None:
        scores = scores + bias_block
    scores = jnp.where(allowed[None], scores, -1e30)
    probs = jnp.exp(scores - log_total)
    probs_low = probs.astype(jnp.bfloat16)
    grad_heads = split_heads(grad_attended, head_count)
    grad_values = product("hqk,qhd->khd", probs_low, grad_heads)
    grad_probs = product("qhd,khd->hqk", grad_heads, value_heads)
    delta = jnp.sum(
        grad_heads.astype(jnp.float32) * split_heads(attended, head_count).astype(jnp.float32),
        axis=-1,
    )
    grad_scores = probs * (grad_probs - delta.T[:, :, None])
    scores_low = grad_scores.astype(jnp.bfloat16)
    grad_query = product("hqk,khd->qhd", scores_low, key_heads)
    grad_keys = product("hqk,qhd->khd", scores_low, query_heads)
    grad_query = grad_query.reshape(query.shape).astype(jnp.bfloat16)
    grad_keys = grad_keys.reshape(key_rows.shape).astype(jnp.bfloat16)
    grad_values = grad_values.reshape(value_rows.shape).astype(jnp.bfloat16)
    return (grad_query, grad_keys, grad_values, grad_scores)


def layer_forward(
    hidden_in, enc_block, allowed_self, allowed_cross, bias_block, weights, reduce_sum
):
    w_query, w_key, w_value, c_query, c_key, c_value, w_gate, w_up, w_out, c_out, w_down, gains = (
        weights
    )
    head_count = w_query.shape[1] // HEAD
    resid_zero = hidden_in.astype(jnp.float32)
    normed_one = rms_norm(resid_zero, gains[0]).astype(jnp.bfloat16)
    self_query = product("rd,di->ri", normed_one, w_query).astype(jnp.bfloat16)
    self_keys = product("rd,di->ri", normed_one, w_key).astype(jnp.bfloat16)
    self_values = product("rd,di->ri", normed_one, w_value).astype(jnp.bfloat16)
    self_out, self_lse = attend(
        self_query, self_keys, self_values, bias_block, allowed_self, head_count
    )
    resid_one = resid_zero + reduce_sum(((self_out, w_out),))
    normed_two = rms_norm(resid_one, gains[1]).astype(jnp.bfloat16)
    cross_query = product("rd,di->ri", normed_two, c_query).astype(jnp.bfloat16)
    cross_keys = product("ed,di->ei", enc_block, c_key).astype(jnp.bfloat16)
    cross_values = product("ed,di->ei", enc_block, c_value).astype(jnp.bfloat16)
    cross_out, cross_lse = attend(
        cross_query, cross_keys, cross_values, None, allowed_cross, head_count
    )
    resid_two = resid_one + reduce_sum(((cross_out, c_out),))
    normed_three = rms_norm(resid_two, gains[2]).astype(jnp.bfloat16)
    gate_pre = product("rd,df->rf", normed_three, w_gate)
    up_pre = product("rd,df->rf", normed_three, w_up)
    hidden = (gelu_tanh(gate_pre) * up_pre).astype(jnp.bfloat16)
    result = resid_two + reduce_sum(((hidden, w_down),))
    saved_state = (
        normed_one,
        self_query,
        self_keys,
        self_values,
        self_lse,
        self_out,
        resid_one,
        normed_two,
        cross_query,
        cross_keys,
        cross_values,
        cross_lse,
        cross_out,
        resid_two,
        normed_three,
        gate_pre,
        up_pre,
        hidden,
    )
    return (result, saved_state)


def layer_backward(
    grad_out,
    hidden_in,
    enc_block,
    saved_state,
    allowed_self,
    allowed_cross,
    bias_block,
    spread,
    weights,
    reduce_sum,
):
    w_query, w_key, w_value, c_query, c_key, c_value, w_gate, w_up, w_out, c_out, w_down, gains = (
        weights
    )
    (
        normed_one,
        self_query,
        self_keys,
        self_values,
        self_lse,
        self_out,
        resid_one,
        normed_two,
        cross_query,
        cross_keys,
        cross_values,
        cross_lse,
        cross_out,
        resid_two,
        normed_three,
        gate_pre,
        up_pre,
        hidden,
    ) = saved_state
    head_count = w_query.shape[1] // HEAD
    resid_zero = hidden_in.astype(jnp.float32)
    grad_three_low = grad_out.astype(jnp.bfloat16)
    grad_down = product("rf,rd->fd", hidden, grad_three_low)
    grad_hidden = product("rd,fd->rf", grad_three_low, w_down)
    gelu_value, gelu_pull = jax.vjp(gelu_tanh, gate_pre)
    grad_gate_pre = gelu_pull(grad_hidden * up_pre)[0].astype(jnp.bfloat16)
    grad_up_pre = (grad_hidden * gelu_value).astype(jnp.bfloat16)
    grad_gate = product("rd,rf->df", normed_three, grad_gate_pre)
    grad_up = product("rd,rf->df", normed_three, grad_up_pre)
    grad_normed = reduce_sum(((grad_gate_pre, w_gate.T), (grad_up_pre, w_up.T)))
    back_three, gain_three = norm_back(resid_two, gains[2], grad_normed)
    grad_two = grad_out + back_three
    grad_two_low = grad_two.astype(jnp.bfloat16)
    grad_c_out = product("ri,rd->id", cross_out, grad_two_low)
    grad_cross = product("rd,id->ri", grad_two_low, c_out).astype(jnp.bfloat16)
    grad_cross_query, grad_cross_keys, grad_cross_values, _ = attend_back(
        grad_cross,
        cross_query,
        cross_keys,
        cross_values,
        None,
        allowed_cross,
        cross_lse,
        cross_out,
        head_count,
    )
    grad_c_query = product("rd,ri->di", normed_two, grad_cross_query)
    grad_c_key = product("ed,ei->di", enc_block, grad_cross_keys)
    grad_c_value = product("ed,ei->di", enc_block, grad_cross_values)
    grad_enc = product("ei,di->ed", grad_cross_keys, c_key) + product(
        "ei,di->ed", grad_cross_values, c_value
    )
    grad_normed = reduce_sum(((grad_cross_query, c_query.T),))
    back_two, gain_two = norm_back(resid_one, gains[1], grad_normed)
    grad_one = grad_two + back_two
    grad_one_low = grad_one.astype(jnp.bfloat16)
    grad_w_out = product("ri,rd->id", self_out, grad_one_low)
    grad_self = product("rd,id->ri", grad_one_low, w_out).astype(jnp.bfloat16)
    grad_query, grad_keys, grad_values, grad_scores = attend_back(
        grad_self,
        self_query,
        self_keys,
        self_values,
        bias_block,
        allowed_self,
        self_lse,
        self_out,
        head_count,
    )
    grad_bucket = bias_grad(grad_scores, spread)
    grad_w_query = product("rd,ri->di", normed_one, grad_query)
    grad_w_key = product("rd,ri->di", normed_one, grad_keys)
    grad_w_value = product("rd,ri->di", normed_one, grad_values)
    grad_normed = reduce_sum(
        ((grad_query, w_query.T), (grad_keys, w_key.T), (grad_values, w_value.T))
    )
    back_one, gain_one = norm_back(resid_zero, gains[0], grad_normed)
    grad_input = grad_one + back_one
    grads = (
        grad_w_query,
        grad_w_key,
        grad_w_value,
        grad_c_query,
        grad_c_key,
        grad_c_value,
        grad_gate,
        grad_up,
        grad_w_out,
        grad_c_out,
        grad_down,
        jnp.stack([gain_one, gain_two, gain_three]),
        grad_bucket,
    )
    return (grad_input, grad_enc, grads)


def zero_grads(inner_width, hidden_width, head_count):
    return (
        (jnp.zeros((D, inner_width), jnp.float32),) * 6
        + (jnp.zeros((D, hidden_width), jnp.float32),) * 2
        + (jnp.zeros((inner_width, D), jnp.float32),) * 2
        + (
            jnp.zeros((hidden_width, D), jnp.float32),
            jnp.zeros((3, D), jnp.float32),
            jnp.zeros((BUCKETS, head_count), jnp.float32),
        )
    )


def unpack_weights(inner_group, outer_group):
    w_query, w_key, w_value, c_query, c_key, c_value, w_gate, w_up, table = [
        piece[0] for piece in inner_group
    ]
    w_out, c_out, w_down, gains = [piece[0] for piece in outer_group]
    weights = (
        w_query,
        w_key,
        w_value,
        c_query,
        c_key,
        c_value,
        w_gate,
        w_up,
        w_out,
        c_out,
        w_down,
        gains.astype(jnp.float32),
    )
    return (weights, table.astype(jnp.float32))


def store(buffer, value, index, valid_flag):
    return buffer.at[index].set(jnp.where(valid_flag, value, buffer[index]))


def body(
    layer_input,
    enc_states,
    out_grad,
    dec_seg,
    enc_seg,
    buckets,
    sa_q,
    sa_k,
    sa_v,
    sa_o,
    ca_q,
    ca_k,
    ca_v,
    ca_o,
    ff_gate,
    ff_up,
    ff_down,
    norm_gains,
    rel_table,
):
    section_count = lax.axis_size("pipe")
    section_id = lax.axis_index("pipe")
    micro_count = layer_input.shape[0]
    row_count = layer_input.shape[1]
    spread = offset_spread(buckets, row_count)
    inner_group = (
        lax.all_gather(sa_q, "dp", axis=1, tiled=True),
        lax.all_gather(sa_k, "dp", axis=1, tiled=True),
        lax.all_gather(sa_v, "dp", axis=1, tiled=True),
        lax.all_gather(ca_q, "dp", axis=1, tiled=True),
        lax.all_gather(ca_k, "dp", axis=1, tiled=True),
        lax.all_gather(ca_v, "dp", axis=1, tiled=True),
        lax.all_gather(ff_gate, "dp", axis=1, tiled=True),
        lax.all_gather(ff_up, "dp", axis=1, tiled=True),
        lax.all_gather(rel_table, "dp", axis=1, tiled=True),
    )
    outer_group = (
        lax.all_gather(sa_o, "dp", axis=2, tiled=True),
        lax.all_gather(ca_o, "dp", axis=2, tiled=True),
        lax.all_gather(ff_down, "dp", axis=2, tiled=True),
        lax.all_gather(norm_gains, "dp", axis=2, tiled=True),
    )
    weights, table_float = unpack_weights(inner_group, outer_group)
    bias_block = bias_from_table(spread, table_float, row_count)
    tick_count = micro_count + section_count - 1
    received = jnp.zeros(layer_input.shape[1:], jnp.bfloat16)
    outputs_all = jnp.zeros(layer_input.shape, jnp.bfloat16)
    saved_all = None
    for tick_id in range(tick_count):
        micro_id = tick_id - section_id
        valid_flag = (micro_id >= 0) & (micro_id < micro_count)
        micro_safe = jnp.clip(micro_id, 0, micro_count - 1)
        hidden_in = jnp.where(section_id == 0, layer_input[micro_safe], received)
        allowed_self, allowed_cross = build_masks(dec_seg[micro_safe], enc_seg[micro_safe])
        result, saved_state = layer_forward(
            hidden_in,
            enc_states[micro_safe],
            allowed_self,
            allowed_cross,
            bias_block,
            weights,
            forward_sum,
        )
        result_low = result.astype(jnp.bfloat16)
        saved_state = (hidden_in,) + saved_state
        if saved_all is None:
            saved_all = jax.tree.map(
                lambda a: jnp.zeros((micro_count,) + a.shape, a.dtype), saved_state
            )
        saved_all = jax.tree.map(
            lambda a, b: store(a, b, micro_safe, valid_flag), saved_all, saved_state
        )
        outputs_all = store(outputs_all, result_low, micro_safe, valid_flag)
        received = passed_along(result_low, "pipe", 1)
    inner_group = (
        lax.all_gather(sa_q, "dp", axis=1, tiled=True),
        lax.all_gather(sa_k, "dp", axis=1, tiled=True),
        lax.all_gather(sa_v, "dp", axis=1, tiled=True),
        lax.all_gather(ca_q, "dp", axis=1, tiled=True),
        lax.all_gather(ca_k, "dp", axis=1, tiled=True),
        lax.all_gather(ca_v, "dp", axis=1, tiled=True),
        lax.all_gather(ff_gate, "dp", axis=1, tiled=True),
        lax.all_gather(ff_up, "dp", axis=1, tiled=True),
        lax.all_gather(rel_table, "dp", axis=1, tiled=True),
    )
    outer_group = (
        lax.all_gather(sa_o, "dp", axis=2, tiled=True),
        lax.all_gather(ca_o, "dp", axis=2, tiled=True),
        lax.all_gather(ff_down, "dp", axis=2, tiled=True),
        lax.all_gather(norm_gains, "dp", axis=2, tiled=True),
    )
    weights, table_float = unpack_weights(inner_group, outer_group)
    bias_block = bias_from_table(spread, table_float, row_count)
    grads_total = zero_grads(sa_q.shape[2], ff_gate.shape[2], rel_table.shape[2])
    in_grads_all = jnp.zeros(layer_input.shape, jnp.float32)
    enc_all = jnp.zeros(enc_states.shape, jnp.float32)
    received = jnp.zeros(layer_input.shape[1:], jnp.bfloat16)
    for tick_id in range(tick_count):
        micro_id = tick_id - (section_count - 1 - section_id)
        valid_flag = (micro_id >= 0) & (micro_id < micro_count)
        micro_safe = jnp.clip(micro_id, 0, micro_count - 1)
        upstream = jnp.where(
            section_id == section_count - 1, out_grad[micro_safe], received
        ).astype(jnp.float32)
        saved_state = jax.tree.map(lambda a: a[micro_safe], saved_all)
        allowed_self, allowed_cross = build_masks(dec_seg[micro_safe], enc_seg[micro_safe])
        grad_input, grad_enc, grads = layer_backward(
            upstream,
            saved_state[0],
            enc_states[micro_safe],
            saved_state[1:],
            allowed_self,
            allowed_cross,
            bias_block,
            spread,
            weights,
            backward_sum,
        )
        grads_total = jax.tree.map(
            lambda a, b: a + jnp.where(valid_flag, b, 0.0), grads_total, grads
        )
        in_grads_all = store(in_grads_all, grad_input, micro_safe, valid_flag)
        enc_all = store(enc_all, grad_enc, micro_safe, valid_flag)
        received = passed_along(grad_input.astype(jnp.bfloat16), "pipe", -1)
    enc_part = lax.psum_scatter(
        enc_all.astype(jnp.bfloat16), "tensor", scatter_dimension=2, tiled=True
    ).astype(jnp.float32)
    (
        grad_w_query,
        grad_w_key,
        grad_w_value,
        grad_c_query,
        grad_c_key,
        grad_c_value,
        grad_gate,
        grad_up,
        grad_w_out,
        grad_c_out,
        grad_down,
        grad_gains,
        grad_table,
    ) = grads_total
    inner_sums = (
        lax.psum_scatter(
            grad_w_query[None].astype(jnp.bfloat16), "dp", scatter_dimension=1, tiled=True
        ).astype(jnp.float32),
        lax.psum_scatter(
            grad_w_key[None].astype(jnp.bfloat16), "dp", scatter_dimension=1, tiled=True
        ).astype(jnp.float32),
        lax.psum_scatter(
            grad_w_value[None].astype(jnp.bfloat16), "dp", scatter_dimension=1, tiled=True
        ).astype(jnp.float32),
        lax.psum_scatter(
            grad_c_query[None].astype(jnp.bfloat16), "dp", scatter_dimension=1, tiled=True
        ).astype(jnp.float32),
        lax.psum_scatter(
            grad_c_key[None].astype(jnp.bfloat16), "dp", scatter_dimension=1, tiled=True
        ).astype(jnp.float32),
        lax.psum_scatter(
            grad_c_value[None].astype(jnp.bfloat16), "dp", scatter_dimension=1, tiled=True
        ).astype(jnp.float32),
        lax.psum_scatter(
            grad_gate[None].astype(jnp.bfloat16), "dp", scatter_dimension=1, tiled=True
        ).astype(jnp.float32),
        lax.psum_scatter(
            grad_up[None].astype(jnp.bfloat16), "dp", scatter_dimension=1, tiled=True
        ).astype(jnp.float32),
        lax.psum_scatter(
            grad_table[None].astype(jnp.bfloat16), "dp", scatter_dimension=1, tiled=True
        ).astype(jnp.float32),
    )
    outer_sums = (
        lax.psum_scatter(
            grad_w_out[None].astype(jnp.bfloat16), "dp", scatter_dimension=2, tiled=True
        ).astype(jnp.float32),
        lax.psum_scatter(
            grad_c_out[None].astype(jnp.bfloat16), "dp", scatter_dimension=2, tiled=True
        ).astype(jnp.float32),
        lax.psum_scatter(
            grad_down[None].astype(jnp.bfloat16), "dp", scatter_dimension=2, tiled=True
        ).astype(jnp.float32),
        lax.psum_scatter(
            grad_gains[None].astype(jnp.bfloat16), "dp", scatter_dimension=2, tiled=True
        ).astype(jnp.float32),
    )
    return (
        outputs_all[None],
        in_grads_all[None],
        enc_part[None],
        inner_sums[0],
        inner_sums[1],
        inner_sums[2],
        outer_sums[0],
        inner_sums[3],
        inner_sums[4],
        inner_sums[5],
        outer_sums[1],
        inner_sums[6],
        inner_sums[7],
        outer_sums[2],
        outer_sums[3],
        inner_sums[8],
    )


def solution(mesh):
    placed = (
        P(None, "dp", None),
        P(None, "dp", None),
        P(None, "dp", None),
        P(None, "dp"),
        P(None, "dp"),
        P(),
        P("pipe", "dp", "tensor"),
        P("pipe", "dp", "tensor"),
        P("pipe", "dp", "tensor"),
        P("pipe", "tensor", "dp"),
        P("pipe", "dp", "tensor"),
        P("pipe", "dp", "tensor"),
        P("pipe", "dp", "tensor"),
        P("pipe", "tensor", "dp"),
        P("pipe", "dp", "tensor"),
        P("pipe", "dp", "tensor"),
        P("pipe", "tensor", "dp"),
        P("pipe", None, "dp"),
        P("pipe", "dp", "tensor"),
    )
    return jax.shard_map(
        body,
        mesh=mesh,
        in_specs=placed,
        out_specs=(
            P("pipe", None, "dp", None),
            P("pipe", None, "dp", None),
            P("pipe", None, "dp", "tensor"),
            P("pipe", "dp", "tensor"),
            P("pipe", "dp", "tensor"),
            P("pipe", "dp", "tensor"),
            P("pipe", "tensor", "dp"),
            P("pipe", "dp", "tensor"),
            P("pipe", "dp", "tensor"),
            P("pipe", "dp", "tensor"),
            P("pipe", "tensor", "dp"),
            P("pipe", "dp", "tensor"),
            P("pipe", "dp", "tensor"),
            P("pipe", "tensor", "dp"),
            P("pipe", None, "dp"),
            P("pipe", "dp", "tensor"),
        ),
        check_vma=False,
    )
```

profile of v0, /device:TPU:0, one launch (start us, length us, event | category | flops | bytes accessed | tf_op | source)
XLA Modules:
  0.0 1292.1 jit_solution(11957307132988884322)
XLA Ops:
  8.2 16.3 %all_gather.106 = bf16[1,3,768]{1,0,2:T(2,128)(2,1)S(1)} all-gather(bf16[1,3,192]{1,0,2:T(2,128)(2,1)S(1)} %copy.202), channel_id=1, replica_groups=mesh['pipe'=2,'tensor'=4,'dp'=4] {'dp'}, dimensions={2}, use_global_device_ids=true | all-gather | bytes 5760 | tf_op jit(solution)/shard_map/all_gather | solution.py:389
  32.6 15.4 %all_gather.107 = bf16[1,768,192]{2,1,0:T(8,128)(2,1)S(1)} all-gather(bf16[1,192,192]{2,1,0:T(8,128)(2,1)S(1)} %copy-done.270), channel_id=1, replica_groups=mesh['pipe'=2,'tensor'=4,'dp'=4] {'dp'}, dimensions={1}, use_global_device_ids=true | all-gather | bytes 368640 | tf_op jit(solution)/shard_map/all_gather | solution.py:377
  70.1 15.3 %all_gather.108 = bf16[1,768,192]{2,1,0:T(8,128)(2,1)S(1)} all-gather(bf16[1,192,192]{2,1,0:T(8,128)(2,1)S(1)} %copy-done.271), channel_id=1, replica_groups=mesh['pipe'=2,'tensor'=4,'dp'=4] {'dp'}, dimensions={1}, use_global_device_ids=true | all-gather | bytes 368640 | tf_op jit(solution)/shard_map/all_gather | solution.py:375
  104.8 17.3 %all_gather.111 = bf16[1,192,768]{1,0,2:T(2,128)(2,1)S(1)} all-gather(bf16[1,192,192]{1,0,2:T(2,128)(2,1)S(1)} %copy.207), channel_id=1, replica_groups=mesh['pipe'=2,'tensor'=4,'dp'=4] {'dp'}, dimensions={2}, use_global_device_ids=true | all-gather | bytes 368640 | tf_op jit(solution)/shard_map/all_gather | solution.py:386
  126.6 15.3 %all_gather.113 = bf16[1,768,192]{2,1,0:T(8,128)(2,1)S(1)} all-gather(bf16[1,192,192]{2,1,0:T(8,128)(2,1)S(1)} %copy-done.273), channel_id=1, replica_groups=mesh['pipe'=2,'tensor'=4,'dp'=4] {'dp'}, dimensions={1}, use_global_device_ids=true | all-gather | bytes 368640 | tf_op jit(solution)/shard_map/all_gather | solution.py:380
  141.9 15.4 %all_gather.114 = bf16[1,768,192]{2,1,0:T(8,128)(2,1)S(1)} all-gather(bf16[1,192,192]{2,1,0:T(8,128)(2,1)S(1)} %copy-done.274), channel_id=1, replica_groups=mesh['pipe'=2,'tensor'=4,'dp'=4] {'dp'}, dimensions={1}, use_global_device_ids=true | all-gather | bytes 368640 | tf_op jit(solution)/shard_map/all_gather | solution.py:378
  173.9 16.4 %all_gather.116 = bf16[1,192,768]{1,0,2:T(2,128)(2,1)} all-gather(bf16[1,192,192]{1,0,2:T(2,128)(2,1)S(1)} %copy.209), channel_id=1, replica_groups=mesh['pipe'=2,'tensor'=4,'dp'=4] {'dp'}, dimensions={2}, use_global_device_ids=true | all-gather | bytes 368640 | tf_op jit(solution)/shard_map/all_gather | solution.py:387
  223.9 15.7 %all_gather.118 = bf16[1,768,512]{2,1,0:T(8,128)(2,1)S(1)} all-gather(bf16[1,192,512]{2,1,0:T(8,128)(2,1)S(1)} %copy-done.260), channel_id=1, replica_groups=mesh['pipe'=2,'tensor'=4,'dp'=4] {'dp'}, dimensions={1}, use_global_device_ids=true | all-gather | bytes 983040 | tf_op jit(solution)/shard_map/all_gather | solution.py:381
  239.6 17.5 %all_gather.119 = bf16[1,768,512]{2,1,0:T(8,128)(2,1)S(1)} all-gather(bf16[1,192,512]{2,1,0:T(8,128)(2,1)S(1)} %copy-done.261), channel_id=1, replica_groups=mesh['pipe'=2,'tensor'=4,'dp'=4] {'dp'}, dimensions={1}, use_global_device_ids=true | all-gather | bytes 983040 | tf_op jit(solution)/shard_map/all_gather | solution.py:382
  281.0 16.6 %all_gather.120 = bf16[1,512,768]{1,2,0:T(8,128)(2,1)} all-gather(bf16[1,512,192]{1,2,0:T(8,128)(2,1)} %param.167), channel_id=1, replica_groups=mesh['pipe'=2,'tensor'=4,'dp'=4] {'dp'}, dimensions={2}, use_global_device_ids=true | all-gather | bytes 983040 | tf_op jit(solution)/shard_map/all_gather | solution.py:388
  375.4 17.5 %reduce-scatter.58.cloned.1.call-done = f32[128,192]{0,1:T(8,128)} async-done(((f32[128,768]{0,1:T(8,128)}), f32[128,192]{0,1:T(8,128)}) %reduce-scatter.58.cloned.1.call-update) | async-done | bytes 98320 | tf_op jit(solution)/shard_map/reduce_scatter | solution.py:85
  418.8 16.2 %reduce-scatter.60.cloned.1.call-done = f32[128,192]{0,1:T(8,128)} async-done(((f32[128,768]{0,1:T(8,128)}), f32[128,192]{0,1:T(8,128)}) %reduce-scatter.60.cloned.1.call-update) | async-done | bytes 98320 | tf_op jit(solution)/shard_map/reduce_scatter | solution.py:85
  461.3 17.3 %reduce-scatter.62.cloned.1.call-done = f32[128,192]{0,1:T(8,128)} async-done(((f32[128,768]{0,1:T(8,128)}), f32[128,192]{0,1:T(8,128)}) %reduce-scatter.62.cloned.1.call-update) | async-done | bytes 98320 | tf_op jit(solution)/shard_map/reduce_scatter | solution.py:85
  510.1 16.5 %reduce-scatter.64.cloned.1.call-done = f32[128,192]{0,1:T(8,128)} async-done(((f32[128,768]{0,1:T(8,128)}), f32[128,192]{0,1:T(8,128)}) %reduce-scatter.64.cloned.1.call-update) | async-done | bytes 98320 | tf_op jit(solution)/shard_map/reduce_scatter | solution.py:85
  552.2 16.5 %reduce-scatter.66.cloned.1.call-done = f32[128,192]{0,1:T(8,128)} async-done(((f32[128,768]{0,1:T(8,128)}), f32[128,192]{0,1:T(8,128)}) %reduce-scatter.66.cloned.1.call-update) | async-done | bytes 98320 | tf_op jit(solution)/shard_map/reduce_scatter | solution.py:85
  594.0 20.1 %reduce-scatter.70.cloned.1.call-done = bf16[128,192]{0,1:T(8,128)(2,1)} async-done(((bf16[128,768]{0,1:T(8,128)(2,1)}), bf16[128,192]{0,1:T(8,128)(2,1)}) %reduce-scatter.70.cloned.1.call-update) | async-done | bytes 49168 | tf_op jit(solution)/shard_map/reduce_scatter | solution.py:90
  631.2 20.8 %reduce-scatter.72.cloned.1.call-done = bf16[128,192]{0,1:T(8,128)(2,1)} async-done(((bf16[128,768]{0,1:T(8,128)(2,1)}), bf16[128,192]{0,1:T(8,128)(2,1)}) %reduce-scatter.72.cloned.1.call-update) | async-done | bytes 49168 | tf_op jit(solution)/shard_map/reduce_scatter | solution.py:90
  670.1 21.8 %reduce-scatter.74.cloned.1.call-done = bf16[128,192]{0,1:T(8,128)(2,1)} async-done(((bf16[128,768]{0,1:T(8,128)(2,1)}), bf16[128,192]{0,1:T(8,128)(2,1)}) %reduce-scatter.74.cloned.1.call-update) | async-done | bytes 49168 | tf_op jit(solution)/shard_map/reduce_scatter | solution.py:90
  713.8 21.4 %reduce-scatter.76.cloned.1.call-done = bf16[128,192]{0,1:T(8,128)(2,1)} async-done(((bf16[128,768]{0,1:T(8,128)(2,1)}), bf16[128,192]{0,1:T(8,128)(2,1)}) %reduce-scatter.76.cloned.1.call-update) | async-done | bytes 49168 | tf_op jit(solution)/shard_map/reduce_scatter | solution.py:90
  754.2 21.2 %reduce-scatter.78.cloned.1.call-done = bf16[128,192]{0,1:T(8,128)(2,1)} async-done(((bf16[128,768]{0,1:T(8,128)(2,1)}), bf16[128,192]{0,1:T(8,128)(2,1)}) %reduce-scatter.78.cloned.1.call-update) | async-done | bytes 49168 | tf_op jit(solution)/shard_map/reduce_scatter | solution.py:90
  793.5 21.9 %reduce-scatter.80.cloned.1.call-done = bf16[128,192]{0,1:T(8,128)(2,1)} async-done(((bf16[128,768]{0,1:T(8,128)(2,1)}), bf16[128,192]{0,1:T(8,128)(2,1)}) %reduce-scatter.80.cloned.1.call-update) | async-done | bytes 49168 | tf_op jit(solution)/shard_map/reduce_scatter | solution.py:90
  836.2 22.4 %reduce-scatter.82.cloned.1.call-done = bf16[128,192]{0,1:T(8,128)(2,1)} async-done(((bf16[128,768]{0,1:T(8,128)(2,1)}), bf16[128,192]{0,1:T(8,128)(2,1)}) %reduce-scatter.82.cloned.1.call-update) | async-done | bytes 49168 | tf_op jit(solution)/shard_map/reduce_scatter | solution.py:90
  873.6 24.0 %reduce-scatter.84.cloned.1.call-done = bf16[128,192]{0,1:T(8,128)(2,1)} async-done(((bf16[128,768]{0,1:T(8,128)(2,1)}), bf16[128,192]{0,1:T(8,128)(2,1)}) %reduce-scatter.84.cloned.1.call-update) | async-done | bytes 49168 | tf_op jit(solution)/shard_map/reduce_scatter | solution.py:90
  1081.8 19.9 %all-reduce.10.cloned.1.call-done = bf16[2,256,768]{1,0,2:T(2,128)(2,1)} async-done(((bf16[2,256,768]{1,0,2:T(2,128)(2,1)}), bf16[2,256,768]{1,0,2:T(2,128)(2,1)}) %all-reduce.10.cloned.1.call-update) | async-done | bytes 786448
  1103.5 20.5 %reduce-scatter.110.cloned.1.call-done = bf16[192,3]{1,0:T(8,128)(2,1)} async-done(((bf16[768,3]{1,0:T(8,128)(2,1)}), bf16[192,3]{1,0:T(8,128)(2,1)}) %reduce-scatter.110.cloned.1.call-update) | async-done | bytes 1168
  1125.8 20.1 %reduce-scatter.92.cloned.1.call-done = bf16[192,192]{1,0:T(8,128)(2,1)} async-done(((bf16[768,192]{1,0:T(8,128)(2,1)}), bf16[192,192]{1,0:T(8,128)(2,1)}) %reduce-scatter.92.cloned.1.call-update) | async-done | bytes 73744
  1147.8 19.2 %reduce-scatter.94.cloned.1.call-done = bf16[192,192]{1,0:T(8,128)(2,1)} async-done(((bf16[768,192]{1,0:T(8,128)(2,1)}), bf16[192,192]{1,0:T(8,128)(2,1)}) %reduce-scatter.94.cloned.1.call-update) | async-done | bytes 73744
  1169.0 19.2 %reduce-scatter.96.cloned.1.call-done = bf16[192,192]{1,0:T(8,128)(2,1)} async-done(((bf16[768,192]{1,0:T(8,128)(2,1)}), bf16[192,192]{1,0:T(8,128)(2,1)}) %reduce-scatter.96.cloned.1.call-update) | async-done | bytes 73744
  1190.1 19.4 %reduce-scatter.98.cloned.1.call-done = bf16[192,192]{1,0:T(8,128)(2,1)} async-done(((bf16[768,192]{1,0:T(8,128)(2,1)}), bf16[192,192]{1,0:T(8,128)(2,1)}) %reduce-scatter.98.cloned.1.call-update) | async-done | bytes 73744
  1211.4 21.9 %reduce-scatter.108.cloned.1.call-done = bf16[192,512]{1,0:T(8,128)(2,1)} async-done(((bf16[768,512]{1,0:T(8,128)(2,1)}), bf16[192,512]{1,0:T(8,128)(2,1)}) %reduce-scatter.108.cloned.1.call-update) | async-done | bytes 196624
  1235.7 22.4 %reduce-scatter.88.cloned.1.call-done = bf16[1,192,512]{2,1,0:T(8,128)(2,1)} async-done(((bf16[1,768,512]{2,1,0:T(8,128)(2,1)}), bf16[1,192,512]{2,1,0:T(8,128)(2,1)}) %reduce-scatter.88.cloned.1.call-update) | async-done | bytes 196624 | tf_op jit(solution)/shard_map/reduce_scatter | solution.py:510
  1259.8 23.3 %reduce-scatter.90.cloned.1.call-done = bf16[1,192,512]{2,1,0:T(8,128)(2,1)} async-done(((bf16[1,768,512]{2,1,0:T(8,128)(2,1)}), bf16[1,192,512]{2,1,0:T(8,128)(2,1)}) %reduce-scatter.90.cloned.1.call-update) | async-done | bytes 196624 | tf_op jit(solution)/shard_map/reduce_scatter | solution.py:513
  (1239 shorter events, 666.7 us)
Async XLA Ops:
  7.2 249.9 %reduce-scatter.52.cloned.1.call-start = ((), (), s32[]{:S(2)}) async-start(), calls=%async_computation.30 | async-start | bytes 491520 | tf_op jit(solution)/shard_map/reduce_scatter | solution.py:85
  126.5 175.7 %reduce-scatter.54.cloned.1.call-start = ((), (), s32[]{:S(2)}) async-start(), calls=%async_computation.31 | async-start | bytes 491520 | tf_op jit(solution)/shard_map/reduce_scatter | solution.py:85
  273.3 71.1 %reduce-scatter.56.cloned.1.call-start = ((), (), s32[]{:S(2)}) async-start(), calls=%async_computation.32 | async-start | bytes 491520 | tf_op jit(solution)/shard_map/reduce_scatter | solution.py:85
  320.3 72.5 %reduce-scatter.58.cloned.1.call-start = ((), (), s32[]{:S(2)}) async-start(), calls=%async_computation.33 | async-start | bytes 491520 | tf_op jit(solution)/shard_map/reduce_scatter | solution.py:85
  357.2 3.8 collective-permute-start
  368.0 67.0 %reduce-scatter.60.cloned.1.call-start = ((), (), s32[]{:S(2)}) async-start(), calls=%async_computation.34 | async-start | bytes 491520 | tf_op jit(solution)/shard_map/reduce_scatter | solution.py:85
  410.2 68.5 %reduce-scatter.62.cloned.1.call-start = ((), (), s32[]{:S(2)}) async-start(), calls=%async_computation.35 | async-start | bytes 491520 | tf_op jit(solution)/shard_map/reduce_scatter | solution.py:85
  453.8 72.8 %reduce-scatter.64.cloned.1.call-start = ((), (), s32[]{:S(2)}) async-start(), calls=%async_computation.36 | async-start | bytes 491520 | tf_op jit(solution)/shard_map/reduce_scatter | solution.py:85
  501.7 67.0 %reduce-scatter.66.cloned.1.call-start = ((), (), s32[]{:S(2)}) async-start(), calls=%async_computation.37 | async-start | bytes 491520 | tf_op jit(solution)/shard_map/reduce_scatter | solution.py:85
  543.8 70.3 %reduce-scatter.70.cloned.1.call-start = ((), (), s32[]{:S(2)}) async-start(), calls=%async_computation.39 | async-start | bytes 245760 | tf_op jit(solution)/shard_map/reduce_scatter | solution.py:90
  589.7 62.3 %reduce-scatter.72.cloned.1.call-start = ((), (), s32[]{:S(2)}) async-start(), calls=%async_computation.40 | async-start | bytes 245760 | tf_op jit(solution)/shard_map/reduce_scatter | solution.py:90
  627.6 64.2 %reduce-scatter.74.cloned.1.call-start = ((), (), s32[]{:S(2)}) async-start(), calls=%async_computation.41 | async-start | bytes 245760 | tf_op jit(solution)/shard_map/reduce_scatter | solution.py:90
  667.5 67.8 %reduce-scatter.76.cloned.1.call-start = ((), (), s32[]{:S(2)}) async-start(), calls=%async_computation.42 | async-start | bytes 245760 | tf_op jit(solution)/shard_map/reduce_scatter | solution.py:90
  710.7 64.7 %reduce-scatter.78.cloned.1.call-start = ((), (), s32[]{:S(2)}) async-start(), calls=%async_computation.43 | async-start | bytes 245760 | tf_op jit(solution)/shard_map/reduce_scatter | solution.py:90
  751.1 64.3 %reduce-scatter.80.cloned.1.call-start = ((), (), s32[]{:S(2)}) async-start(), calls=%async_computation.44 | async-start | bytes 245760 | tf_op jit(solution)/shard_map/reduce_scatter | solution.py:90
  791.0 67.6 %reduce-scatter.82.cloned.1.call-start = ((), (), s32[]{:S(2)}) async-start(), calls=%async_computation.45 | async-start | bytes 245760 | tf_op jit(solution)/shard_map/reduce_scatter | solution.py:90
  834.2 63.4 %reduce-scatter.84.cloned.1.call-start = ((), (), s32[]{:S(2)}) async-start(), calls=%async_computation.46 | async-start | bytes 245760 | tf_op jit(solution)/shard_map/reduce_scatter | solution.py:90
  873.2 84.4 %reduce-scatter.86.cloned.1.call-start = ((), (), s32[]{:S(2)}) async-start(), calls=%async_computation.47 | async-start | bytes 245760 | tf_op jit(solution)/shard_map/reduce_scatter | solution.py:90
  912.2 88.0 %reduce-scatter.68.cloned.1.call-start = ((), (), s32[]{:S(2)}) async-start(), calls=%async_computation.38 | async-start | bytes 491520 | tf_op jit(solution)/shard_map/reduce_scatter | solution.py:85
  913.4 152.4 %reduce-scatter.100.cloned.1.call-start = ((), (), s32[]{:S(2)}) async-start(), calls=%async_computation.54 | async-start | bytes 491520
  929.6 137.3 %reduce-scatter.102.cloned.1.call-start = ((), (), s32[]{:S(2)}) async-start(), calls=%async_computation.55 | async-start | bytes 491520
  938.2 134.7 %reduce-scatter.104.cloned.1.call-start = ((), (), s32[]{:S(2)}) async-start(), calls=%async_computation.56 | async-start | bytes 491520
  944.5 131.9 %reduce-scatter.106.cloned.1.call-start = ((), (), s32[]{:S(2)}) async-start(), calls=%async_computation.57 | async-start | bytes 491520
  953.8 147.8 %all-reduce.10.cloned.1.call-start = ((), (), s32[]{:S(2)}) async-start(), calls=%async_computation.60 | async-start | bytes 1572864
  957.1 166.8 %reduce-scatter.110.cloned.1.call-start = ((), (), s32[]{:S(2)}) async-start(), calls=%async_computation.59 | async-start | bytes 245760
  969.0 176.9 %reduce-scatter.92.cloned.1.call-start = ((), (), s32[]{:S(2)}) async-start(), calls=%async_computation.50 | async-start | bytes 491520
  970.8 196.3 %reduce-scatter.94.cloned.1.call-start = ((), (), s32[]{:S(2)}) async-start(), calls=%async_computation.51 | async-start | bytes 491520
  973.3 214.9 %reduce-scatter.96.cloned.1.call-start = ((), (), s32[]{:S(2)}) async-start(), calls=%async_computation.52 | async-start | bytes 491520
  975.8 233.7 %reduce-scatter.98.cloned.1.call-start = ((), (), s32[]{:S(2)}) async-start(), calls=%async_computation.53 | async-start | bytes 491520
  982.0 251.2 %reduce-scatter.108.cloned.1.call-start = ((), (), s32[]{:S(2)}) async-start(), calls=%async_computation.58 | async-start | bytes 983040
  991.7 266.4 %reduce-scatter.88.cloned.1.call-start = ((), (), s32[]{:S(2)}) async-start(), calls=%async_computation.48 | async-start | bytes 983040 | tf_op jit(solution)/shard_map/reduce_scatter | solution.py:510
  1024.8 258.3 %reduce-scatter.90.cloned.1.call-start = ((), (), s32[]{:S(2)}) async-start(), calls=%async_computation.49 | async-start | bytes 983040 | tf_op jit(solution)/shard_map/reduce_scatter | solution.py:513
  (347 other events, 3263.0 us)
Sparse Core Ops, SparseCore 0:
  126.6 25.0 reduce-scatter.51
  273.4 23.6 reduce-scatter.53
  320.5 23.8 reduce-scatter.55
  368.1 24.7 reduce-scatter.57
  410.3 24.7 reduce-scatter.59
  453.9 24.6 reduce-scatter.61
  501.8 24.7 reduce-scatter.63
  543.9 24.7 reduce-scatter.65
  589.8 24.2 reduce-scatter.69
  627.8 24.2 reduce-scatter.71
  667.6 24.2 reduce-scatter.73
  710.9 24.3 reduce-scatter.75
  751.2 24.2 reduce-scatter.77
  791.1 24.2 reduce-scatter.79
  834.3 24.2 reduce-scatter.81
  873.3 24.2 reduce-scatter.83
  912.3 24.2 reduce-scatter.85
  939.8 24.8 reduce-scatter.67
  967.0 20.8 reduce-scatter.99
  990.0 19.0 reduce-scatter.101
  1011.4 19.0 reduce-scatter.103
  1032.7 18.9 reduce-scatter.105
  1054.8 46.8 all-reduce.9
  1104.4 19.5 reduce-scatter.109
  1126.8 19.0 reduce-scatter.91
  1148.0 18.9 reduce-scatter.93
  1169.2 18.9 reduce-scatter.95
  1190.5 19.0 reduce-scatter.97
  1211.9 21.3 reduce-scatter.107
  1235.4 22.6 reduce-scatter.87
  1260.4 22.6 reduce-scatter.89
where the time goes:
time: 1310 us; the launch traced here: 1290 us
  waiting for transfers between devices  461 us (35%)
  blocking collectives  380 us (29%)
  local copies, waits for them, and re-layouts  187 us (14%)
  matrix products  119 us (9%)
  other arithmetic  117 us (9%)
  between operations  20.8 us (2%)
    reduce_scatter x9, waiting for transfers between devices, backward_sum(): lax.psum_scatter(local_terms(operands).astype(jnp.bfloat16), 'tensor', sc...  174 us
    unnamed x42, waiting for transfers between devices  141 us
    reduce_scatter x9, waiting for transfers between devices, forward_sum(): lax.psum_scatter(local_terms(operands), 'tensor', scatter_dimension=1, ti...  98.8 us
    dot_general x114, matrix products, product(): jnp.einsum(form, left_side, right_side, preferred_element_type=jnp.float32)  96.5 us
    all_gather x9, blocking collectives, forward_sum(): return lax.all_gather(part_sum, 'tensor', axis=1, tiled=True)  85.8 us
    unnamed x757, local copies, waits for them, and re-layouts  85 us
    all_gather x9, blocking collectives, backward_sum(): lax.all_gather(part_sum.astype(jnp.bfloat16), 'tensor', axis=1, tiled=True)  78.8 us
    scatter x33, other arithmetic, store(): return buffer.at[index].set(jnp.where(valid_flag, value, buffer[index]))  55.7 us
  transfers between devices with their start and end apart: 35, of which 25 were waited for; matrix products, arithmetic and copies ran while one was open for 21% of the time, Pallas kernels for 0%

commit v1 on v0

v1 whole, which is shorter than its diff:
```python
import functools

import jax
import jax.numpy as jnp
from jax import lax
from jax.experimental import pallas as pl
from jax.experimental.pallas import tpu as pltpu
from jax.sharding import PartitionSpec as P

D = 768
HEAD = 64
BUCKETS = 32
MAXD = 128
EPS = 1e-06
TAIL = 128

F32 = jnp.float32
BF16 = jnp.bfloat16
MESH = pl.DeviceIdType.MESH


def dot_nn(a, b):
    return lax.dot_general(a, b, (((1,), (0,)), ((), ())), preferred_element_type=F32)


def dot_nt(a, b):
    return lax.dot_general(a, b, (((1,), (1,)), ((), ())), preferred_element_type=F32)


def dot_tn(a, b):
    return lax.dot_general(a, b, (((0,), (0,)), ((), ())), preferred_element_type=F32)


def norm_scale(values):
    return lax.rsqrt(jnp.mean(values * values, axis=-1, keepdims=True) + EPS)


def norm_back(values, gain, cotangent):
    scale = norm_scale(values)
    scaled = cotangent * gain
    inner = jnp.mean(scaled * values, axis=-1, keepdims=True)
    back = scale * scaled - values * (scale * scale * scale * inner)
    gain_grad = jnp.sum(cotangent * values * scale, axis=0, keepdims=True)
    return back, gain_grad


def gelu_parts(u):
    root = 0.7978845608028654
    cube = 0.044715
    t = jnp.tanh(root * (u + cube * u * u * u))
    value = 0.5 * u * (1.0 + t)
    slope = 0.5 * (1.0 + t) + 0.5 * u * (1.0 - t * t) * (root * (1.0 + 3.0 * cube * u * u))
    return value, slope


def head_masks(heads):
    lane = lax.broadcasted_iota(jnp.int32, (1, heads * HEAD), 1)
    return [
        ((lane >= h * HEAD) & (lane < (h + 1) * HEAD)).astype(F32).astype(BF16)
        for h in range(heads)
    ]


def spread_heads(values, masks):
    return jnp.concatenate([values * m for m in masks], axis=0)


def join_heads(values, masks):
    rows = values.shape[0] // len(masks)
    total = None
    for h, m in enumerate(masks):
        term = values[h * rows : (h + 1) * rows] * m.astype(F32)
        total = term if total is None else total + term
    return total


def main_kernel(
    dims,
    h_ref,
    enc_ref,
    up_ref,
    w_ref,
    gain_ref,
    bias_ref,
    cmask_ref,
    bmap_ref,
    out_ref,
    ingrad_ref,
    encgrad_ref,
    grad_ref,
    gaingrad_ref,
    table_ref,
    x_in,
    g_in,
    r_one,
    r_two,
    n_one,
    n_two,
    n_three,
    qkv_s,
    so_s,
    p_s,
    cq_s,
    ckv_s,
    co_s,
    pc_s,
    gu_s,
    hid_s,
    send_one,
    recv_one,
    send_two,
    recv_two,
    enc_send,
    enc_own,
    enc_recv,
    sem_send,
    sem_recv,
    sem_enc_send,
    sem_enc_recv,
):
    layers, rows, inner, ff, heads = dims
    half = rows // 2
    t = lax.axis_index("tensor")
    near = t + 1 - 2 * (t % 2)
    far = t + 2 - 4 * ((t // 2) % 2)
    both = far + 1 - 2 * (far % 2)
    peers = (near, far, both)
    masks = head_masks(heads)
    c_q = 3 * ff
    c_so = c_q + 3 * inner
    c_cq = c_q + 4 * inner
    c_ck = c_q + 5 * inner
    c_cv = c_q + 6 * inner
    c_co = c_q + 7 * inner
    c_end = c_q + 8 * inner

    barrier = pltpu.get_barrier_semaphore()
    for peer in peers:
        pl.semaphore_signal(barrier, inc=1, device_id={"tensor": peer}, device_id_type=MESH)
    pl.semaphore_wait(barrier, 3)

    def copy_to(src, dst, sem_a, sem_b, peer):
        return pltpu.make_async_remote_copy(
            src_ref=src,
            dst_ref=dst,
            send_sem=sem_a,
            recv_sem=sem_b,
            device_id={"tensor": peer},
            device_id_type=MESH,
        )

    def all_sum(slot, make_half, cover):
        firsts = []
        for part in range(2):
            value = make_half(part).astype(BF16)
            send_one[slot, part] = value
            copy = copy_to(
                send_one.at[slot, part],
                recv_one.at[slot, part],
                sem_send.at[slot, part],
                sem_recv.at[slot, part],
                near if part == 0 else far,
            )
            copy.start()
            firsts.append(copy)
        if cover is not None:
            cover()
        seconds = []
        for part in range(2):
            firsts[part].wait()
            value = send_one[slot, part].astype(F32) + recv_one[slot, part].astype(F32)
            send_two[slot, part] = value.astype(BF16)
            copy = copy_to(
                send_two.at[slot, part],
                recv_two.at[slot, part],
                sem_send.at[slot, part + 2],
                sem_recv.at[slot, part + 2],
                far if part == 0 else near,
            )
            copy.start()
            seconds.append(copy)
        pieces = []
        for part in range(2):
            seconds[part].wait()
            pieces.append(send_two[slot, part].astype(F32) + recv_two[slot, part].astype(F32))
        return jnp.concatenate(pieces, axis=0)

    x_in[0] = h_ref[...]

    def forward(l, carry):
        x0 = x_in[l].astype(F32)
        n1 = (x0 * norm_scale(x0) * gain_ref[l, 0:1]).astype(BF16)
        n_one[l] = n1
        qkv = dot_nn(n1, w_ref[l, :, c_q:c_so]).astype(BF16)
        qkv_s[l] = qkv
        q = qkv[:, :inner]
        k = qkv[:, inner : 2 * inner]
        v = qkv[:, 2 * inner :]
        e = jnp.exp(dot_nt(spread_heads(q, masks), k) + bias_ref[l])
        p = e * (1.0 / jnp.sum(e, axis=-1, keepdims=True))
        p_s[l] = p
        so_s[l] = join_heads(dot_nn(p.astype(BF16), v), masks).astype(BF16)

        def make_one(part):
            return dot_nt(
                so_s[l, part * half : (part + 1) * half], w_ref[l, :, c_so:c_cq]
            )

        def cover_one():
            ckv_s[l] = dot_nn(enc_ref[...], w_ref[l, :, c_ck:c_co]).astype(BF16)

        x1 = x0 + all_sum(3 * l, make_one, cover_one)
        r_one[l] = x1
        n2 = (x1 * norm_scale(x1) * gain_ref[l, 1:2]).astype(BF16)
        n_two[l] = n2
        cq = dot_nn(n2, w_ref[l, :, c_cq:c_ck]).astype(BF16)
        cq_s[l] = cq
        ckv = ckv_s[l]
        ck = ckv[:, :inner]
        cv = ckv[:, inner:]
        cmask = cmask_ref[...]
        e = jnp.exp(
            dot_nt(spread_heads(cq, masks), ck) + jnp.concatenate([cmask] * heads, axis=0)
        )
        p = e * (1.0 / jnp.sum(e, axis=-1, keepdims=True))
        pc_s[l] = p
        co_s[l] = join_heads(dot_nn(p.astype(BF16), cv), masks).astype(BF16)

        def make_two(part):
            return dot_nt(
                co_s[l, part * half : (part + 1) * half], w_ref[l, :, c_co:c_end]
            )

        x2 = x1 + all_sum(3 * l + 1, make_two, None)
        r_two[l] = x2
        n3 = (x2 * norm_scale(x2) * gain_ref[l, 2:3]).astype(BF16)
        n_three[l] = n3
        gu = dot_nn(n3, w_ref[l, :, 0 : 2 * ff])
        gu_s[l] = gu
        value, _ = gelu_parts(gu[:, :ff])
        hid_s[l] = (value * gu[:, ff:]).astype(BF16)

        def make_three(part):
            return dot_nt(
                hid_s[l, part * half : (part + 1) * half], w_ref[l, :, 2 * ff : 3 * ff]
            )

        result = (x2 + all_sum(3 * l + 2, make_three, None)).astype(BF16)
        out_ref[l] = result
        x_in[l + 1] = result
        return carry

    lax.fori_loop(0, layers, forward, 0)
    g_in[...] = up_ref[...]

    def attend_back(grad, query, keys, values, attended, p):
        gs = spread_heads(grad, masks)
        qs = spread_heads(query, masks)
        delta = jnp.sum(
            gs.astype(F32) * jnp.concatenate([attended.astype(F32)] * heads, axis=0),
            axis=-1,
            keepdims=True,
        )
        ds = p * (dot_nt(gs, values) - delta)
        dsb = ds.astype(BF16)
        grad_query = join_heads(dot_nn(dsb, keys), masks).astype(BF16)
        return grad_query, ds, dsb, gs, qs

    def backward(step, carry):
        l = layers - 1 - step
        base = 3 * layers + 3 * step
        g3 = g_in[...]
        g = g3.astype(F32)
        gu = gu_s[l]
        value, slope = gelu_parts(gu[:, :ff])
        dh = dot_nn(g3, w_ref[l, :, 2 * ff : 3 * ff])
        dgu = jnp.concatenate(
            [(dh * gu[:, ff:] * slope).astype(BF16), (dh * value).astype(BF16)], axis=1
        )

        def make_three(part):
            return dot_nt(dgu[part * half : (part + 1) * half], w_ref[l, :, 0 : 2 * ff])

        def cover_three():
            grad_ref[l, :, 0 : 2 * ff] = dot_tn(n_three[l], dgu).astype(BF16)
            grad_ref[l, :, 2 * ff : 3 * ff] = dot_tn(g3, hid_s[l]).astype(BF16)

        dn = all_sum(base, make_three, cover_three)
        back, gain_three = norm_back(r_two[l], gain_ref[l, 2:3], dn)
        gaingrad_ref[l, 2:3] = gain_three
        g2 = g + back
        g2b = g2.astype(BF16)
        dc = dot_nn(g2b, w_ref[l, :, c_co:c_end]).astype(BF16)
        ckv = ckv_s[l]
        co = co_s[l]
        pc = pc_s[l]
        dcq, _, dsb, gs, qs = attend_back(dc, cq_s[l], ckv[:, :inner], ckv[:, inner:], co, pc)

        def make_two(part):
            return dot_nt(dcq[part * half : (part + 1) * half], w_ref[l, :, c_cq:c_ck])

        def cover_two():
            dck = dot_tn(dsb, qs).astype(BF16)
            dcv = dot_tn(pc.astype(BF16), gs).astype(BF16)
            dckv = jnp.concatenate([dck, dcv], axis=1)
            tsize = D // inner
            for k in range(tsize):
                owner = t if k == 0 else peers[k - 1]
                start = pl.multiple_of(owner * inner, HEAD)
                chunk = dot_nt(dckv, w_ref[l, pl.ds(start, inner), c_ck:c_co])
                if k == 0:
                    enc_own[l] = chunk
                else:
                    enc_send[l, k - 1] = chunk.astype(BF16)
                    copy_to(
                        enc_send.at[l, k - 1],
                        enc_recv.at[l, k - 1],
                        sem_enc_send.at[l, k - 1],
                        sem_enc_recv.at[l, k - 1],
                        peers[k - 1],
                    ).start()
            enc = enc_ref[...]
            block = jnp.concatenate([dot_tn(n_two[l], dcq), dot_tn(enc, dckv)], axis=1)
            grad_ref[l, :, c_cq:c_co] = block.astype(BF16)
            grad_ref[l, :, c_co:c_end] = dot_tn(g2b, co).astype(BF16)

        dn = all_sum(base + 1, make_two, cover_two)
        back, gain_two = norm_back(r_one[l], gain_ref[l, 1:2], dn)
        gaingrad_ref[l, 1:2] = gain_two
        g1 = g2 + back
        g1b = g1.astype(BF16)
        dself = dot_nn(g1b, w_ref[l, :, c_so:c_cq]).astype(BF16)
        qkv = qkv_s[l]
        so = so_s[l]
        ps = p_s[l]
        dq, ds, dsb, gs, qs = attend_back(
            dself, qkv[:, :inner], qkv[:, inner : 2 * inner], qkv[:, 2 * inner :], so, ps
        )
        dk = dot_tn(dsb, qs).astype(BF16)
        dv = dot_tn(ps.astype(BF16), gs).astype(BF16)
        dqkv = jnp.concatenate([dq, dk, dv], axis=1)

        def make_one(part):
            return dot_nt(dqkv[part * half : (part + 1) * half], w_ref[l, :, c_q:c_so])

        def cover_one():
            grad_ref[l, :, c_q:c_cq] = jnp.concatenate(
                [dot_tn(n_one[l], dqkv), dot_tn(g1b, so)], axis=1
            ).astype(BF16)
            bmap = bmap_ref[...]
            for h in range(heads):
                ds_h = ds[h * rows : (h + 1) * rows]
                for b in range(BUCKETS):
                    table_ref[l, h, b : b + 1] = jnp.sum(
                        jnp.where(bmap == b, ds_h, 0.0), axis=0, keepdims=True
                    )

        dn = all_sum(base + 2, make_one, cover_one)
        back, gain_one = norm_back(x_in[l].astype(F32), gain_ref[l, 0:1], dn)
        gaingrad_ref[l, 0:1] = gain_one
        gin = g1 + back
        ingrad_ref[l] = gin
        g_in[...] = gin.astype(BF16)
        return carry

    lax.fori_loop(0, layers, backward, 0)
    for l in range(layers):
        total = enc_own[l]
        for k in range(3):
            copy_to(
                enc_send.at[l, k],
                enc_recv.at[l, k],
                sem_enc_send.at[l, k],
                sem_enc_recv.at[l, k],
                peers[k],
            ).wait()
            total = total + enc_recv[l, k].astype(F32)
        encgrad_ref[l] = total


def run_main(h, enc, up, w, gains, bias, cmask, bmap, inner, ff):
    layers, width = w.shape[0], w.shape[2]
    rows, enc_rows = h.shape[0], enc.shape[0]
    heads = inner // HEAD
    half = rows // 2
    slots = 6 * layers
    vm = pltpu.VMEM
    dims = (layers, rows, inner, ff, heads)
    return pl.pallas_call(
        functools.partial(main_kernel, dims),
        out_shape=(
            jax.ShapeDtypeStruct((layers, rows, D), BF16),
            jax.ShapeDtypeStruct((layers, rows, D), F32),
            jax.ShapeDtypeStruct((layers, enc_rows, inner), F32),
            jax.ShapeDtypeStruct((layers, D, width), BF16),
            jax.ShapeDtypeStruct((layers, 3, D), F32),
            jax.ShapeDtypeStruct((layers, heads, BUCKETS, rows), F32),
        ),
        in_specs=[pl.BlockSpec(memory_space=pltpu.VMEM)] * 8,
        out_specs=(pl.BlockSpec(memory_space=pltpu.VMEM),) * 6,
        scratch_shapes=[
            vm((layers + 1, rows, D), BF16),
            vm((rows, D), BF16),
            vm((layers, rows, D), F32),
            vm((layers, rows, D), F32),
            vm((layers, rows, D), BF16),
            vm((layers, rows, D), BF16),
            vm((layers, rows, D), BF16),
            vm((layers, rows, 3 * inner), BF16),
            vm((layers, rows, inner), BF16),
            vm((layers, heads * rows, rows), F32),
            vm((layers, rows, inner), BF16),
            vm((layers, enc_rows, 2 * inner), BF16),
            vm((layers, rows, inner), BF16),
            vm((layers, heads * rows, enc_rows), F32),
            vm((layers, rows, 2 * ff), F32),
            vm((layers, rows, ff), BF16),
            vm((slots, 2, half, D), BF16),
            vm((slots, 2, half, D), BF16),
            vm((slots, 2, half, D), BF16),
            vm((slots, 2, half, D), BF16),
            vm((layers, 3, enc_rows, inner), BF16),
            vm((layers, enc_rows, inner), F32),
            vm((layers, 3, enc_rows, inner), BF16),
            pltpu.SemaphoreType.DMA((slots, 4)),
            pltpu.SemaphoreType.DMA((slots, 4)),
            pltpu.SemaphoreType.DMA((layers, 3)),
            pltpu.SemaphoreType.DMA((layers, 3)),
        ],
        compiler_params=pltpu.CompilerParams(
            collective_id=0, has_side_effects=True, vmem_limit_bytes=60 * 1024 * 1024
        ),
    )(h, enc, up, w, gains, bias, cmask, bmap)


def body(
    layer_input,
    enc_states,
    out_grad,
    dec_seg,
    enc_seg,
    buckets,
    sa_q,
    sa_k,
    sa_v,
    sa_o,
    ca_q,
    ca_k,
    ca_v,
    ca_o,
    ff_gate,
    ff_up,
    ff_down,
    norm_gains,
    rel_table,
):
    layers = lax.axis_size("pipe")
    dp = lax.axis_size("dp")
    mine = lax.axis_index("pipe")
    rows = layer_input.shape[1]
    inner, ff = sa_q.shape[2], ff_gate.shape[2]
    heads = inner // HEAD
    chunk, table_rows = sa_q.shape[1], rel_table.shape[1]

    def swap(value):
        return lax.ppermute(value, "pipe", [(0, 1), (1, 0)])

    tail = jnp.zeros((chunk, TAIL), BF16)
    tail = lax.dynamic_update_slice(tail, norm_gains[0].T, (0, 0))
    tail = lax.dynamic_update_slice(tail, rel_table[0], (0, 3))
    packed = jnp.concatenate(
        [
            ff_gate[0],
            ff_up[0],
            ff_down[0].T,
            sa_q[0],
            sa_k[0],
            sa_v[0],
            sa_o[0].T,
            ca_q[0],
            ca_k[0],
            ca_v[0],
            ca_o[0].T,
            tail,
        ],
        axis=1,
    )
    width = packed.shape[1]
    w = lax.all_gather(packed, ("pipe", "dp"), axis=0, tiled=True).reshape(layers, D, width)
    tails = w[:, :, width - TAIL :].astype(F32)
    gains = tails[:, :, 0:3].transpose(0, 2, 1)
    table = tails.reshape(layers, dp, chunk, TAIL)[:, :, :table_rows, 3 : 3 + heads]
    table = table.reshape(layers, BUCKETS, heads)

    dec_ids = lax.dynamic_index_in_dim(dec_seg, mine, 0, keepdims=False)
    enc_ids = lax.dynamic_index_in_dim(enc_seg, mine, 0, keepdims=False)
    row_ids = jnp.arange(rows, dtype=jnp.int32)
    allowed_self = (dec_ids[:, None] == dec_ids[None, :]) & (row_ids[None, :] <= row_ids[:, None])
    cmask = jnp.where(dec_ids[:, None] == enc_ids[None, :], 0.0, -1e30).astype(F32)
    distance = jnp.clip(row_ids[:, None] - row_ids[None, :], 0, MAXD - 1)
    bucket_ids = jnp.arange(BUCKETS, dtype=jnp.int32)
    starts = jnp.sum((buckets[None, :] < bucket_ids[1:, None]).astype(jnp.int32), axis=1)
    bmap = jnp.sum((distance[None] >= starts[:, None, None]).astype(jnp.int32), axis=0)
    bias = jnp.sum(
        jnp.where(
            bmap[None, None, None] == bucket_ids[:, None, None, None, None],
            table.transpose(1, 0, 2)[:, :, :, None, None],
            0.0,
        ),
        axis=0,
    )
    bias = jnp.where(allowed_self[None, None], bias, -1e30).reshape(layers, heads * rows, rows)

    h = lax.dynamic_index_in_dim(layer_input, mine, 0, keepdims=False)
    enc = lax.dynamic_index_in_dim(enc_states, mine, 0, keepdims=False)
    up = lax.dynamic_index_in_dim(out_grad, mine, 0, keepdims=False)
    outs, ingrads, encgrads, grads, gain_grads, table_grads = run_main(
        h, enc, up, w, gains, bias, cmask, bmap, inner, ff
    )

    def by_micro(values, sent_type):
        own = lax.dynamic_index_in_dim(values, mine, 0, keepdims=False)
        away = lax.dynamic_index_in_dim(values, 1 - mine, 0, keepdims=False)
        got = swap(away.astype(sent_type)).astype(values.dtype)
        first = jnp.where(mine == 0, own, got)
        second = jnp.where(mine == 0, got, own)
        return jnp.stack([first, second])[None]

    table_grads = jnp.sum(table_grads, axis=-1).transpose(0, 2, 1)
    table_grads = table_grads.reshape(layers, dp, table_rows, heads)
    table_grads = jnp.pad(table_grads, ((0, 0), (0, 0), (0, chunk - table_rows), (0, 0)))
    tail_grads = jnp.concatenate(
        [gain_grads.transpose(0, 2, 1), table_grads.reshape(layers, D, heads)], axis=2
    )
    tail_grads = jnp.pad(tail_grads, ((0, 0), (0, 0), (0, TAIL - 3 - heads))).astype(BF16)
    grads = lax.dynamic_update_slice(grads, tail_grads, (0, 0, width - TAIL))
    summed = lax.psum_scatter(
        grads.reshape(layers * D, width), ("pipe", "dp"), scatter_dimension=0, tiled=True
    ).astype(F32)
    base = 3 * ff

    def cut(index):
        return summed[:, base + index * inner : base + (index + 1) * inner]

    return (
        by_micro(outs, BF16),
        by_micro(ingrads, BF16),
        by_micro(encgrads, BF16),
        cut(0)[None],
        cut(1)[None],
        cut(2)[None],
        cut(3).T[None],
        cut(4)[None],
        cut(5)[None],
        cut(6)[None],
        cut(7).T[None],
        summed[None, :, 0:ff],
        summed[None, :, ff : 2 * ff],
        summed[:, 2 * ff : 3 * ff].T[None],
        summed[:, width - TAIL : width - TAIL + 3].T[None],
        summed[:table_rows, width - TAIL + 3 : width - TAIL + 3 + heads][None],
    )


def solution(mesh):
    inner_spec = P("pipe", "dp", "tensor")
    outer_spec = P("pipe", "tensor", "dp")
    placed = (
        P(None, "dp", None),
        P(None, "dp", None),
        P(None, "dp", None),
        P(None, "dp"),
        P(None, "dp"),
        P(),
        inner_spec,
        inner_spec,
        inner_spec,
        outer_spec,
        inner_spec,
        inner_spec,
        inner_spec,
        outer_spec,
        inner_spec,
        inner_spec,
        outer_spec,
        P("pipe", None, "dp"),
        inner_spec,
    )
    return jax.shard_map(
        body,
        mesh=mesh,
        in_specs=placed,
        out_specs=(
            P("pipe", None, "dp", None),
            P("pipe", None, "dp", None),
            P("pipe", None, "dp", "tensor"),
            inner_spec,
            inner_spec,
            inner_spec,
            outer_spec,
            inner_spec,
            inner_spec,
            inner_spec,
            outer_spec,
            inner_spec,
            inner_spec,
            outer_spec,
            P("pipe", None, "dp"),
            inner_spec,
        ),
        check_vma=False,
    )
```

time: 1310 us -> 455 us (0.35); the launches traced: 1290 us -> 454 us
  blocking collectives: 380 us -> 0 us
  waiting for transfers between devices: 461 us -> 280 us
  local copies, waits for them, and re-layouts: 187 us -> 19.9 us
  Pallas kernels: 0 us -> 130 us
  matrix products: 119 us -> 0 us
  other arithmetic: 117 us -> 9.43 us
    all_gather x31 -> x0, blocking collectives: 368 us -> none  [the longest x9 85.8 us: forward_sum(): return lax.all_gather(part_sum, 'tensor', axis=1, tiled=True)]
    unnamed x42 -> x2, waiting for transfers between devices: 141 us -> 0.03 us
    reduce_scatter x20 -> x1, waiting for transfers between devices: 318 us -> 186 us  [body(): lax.psum_scatter(grads.reshape(layers * D, width), ('pipe', 'dp'), scatte...]
    pallas_call x0 -> x1, Pallas kernels: none -> 130 us  [run_main(): pl.pallas_call(functools.partial(main_kernel, dims), out_shape=(jax.Shape...]
    dot_general x145 -> x0, matrix products: 119 us -> none  [the longest x114 96.5 us: product(): jnp.einsum(form, left_side, right_side, preferred_element_type=jnp.float32)]
    all_gather x0 -> x1, waiting for transfers between devices: none -> 93.5 us  [body(): lax.all_gather(packed, ('pipe', 'dp'), axis=0, tiled=True)]
    unnamed x757 -> x30, local copies, waits for them, and re-layouts: 85 us -> 8.32 us
    scatter x33 -> x0, other arithmetic: 55.7 us -> none  [store(): return buffer.at[index].set(jnp.where(valid_flag, value, buffer[index]))]
  transfers between devices with their start and end apart: 35 -> 5, of which waited for: 25 -> 3; matrix products, arithmetic and copies ran while one was open for 21% -> 1% of each run, Pallas kernels for 0% -> 0%
where the time goes in v1:
time: 455 us; the launch traced here: 454 us
  waiting for transfers between devices  280 us (62%)
  Pallas kernels  130 us (29%)
  local copies, waits for them, and re-layouts  19.9 us (4%)
  between operations  14.4 us (3%)
  other arithmetic  9.43 us (2%)
    reduce_scatter x1, waiting for transfers between devices, body(): lax.psum_scatter(grads.reshape(layers * D, width), ('pipe', 'dp'), scatte...  186 us
    pallas_call x1, Pallas kernels, run_main(): pl.pallas_call(functools.partial(main_kernel, dims), out_shape=(jax.Shape...  130 us
    all_gather x1, waiting for transfers between devices, body(): lax.all_gather(packed, ('pipe', 'dp'), axis=0, tiled=True)  93.5 us
  transfers between devices with their start and end apart: 5, of which 3 were waited for; matrix products, arithmetic and copies ran while one was open for 1% of the time, Pallas kernels for 0%

profile of v1, /device:TPU:0, one launch (start us, length us, event | category | flops | bytes accessed | tf_op | source)
XLA Modules:
  0.0 454.3 jit_solution(6094499033211991293)
XLA Ops:
  7.3 0.9 copy.79
  8.2 0.8 copy.80
  8.9 1.0 copy.77
  9.9 1.0 copy.78
  11.0 0.5 dynamic_update_slice.10
  11.5 3.3 concatenate.7
  15.2 0.8 dynamic-slice_bitcast_fusion.enc_ref
  16.0 0.8 dynamic-slice_bitcast_fusion.2
  17.1 0.7 compare_select_fusion.cmask_ref
  18.2 93.5 %all-gather.2.cloned.1.call-done = bf16[1536,3200]{1,0:T(8,128)(2,1)} async-done(((bf16[192,3200]{1,0:T(8,128)(2,1)}), bf16[1536,3200]{1,0:T(8,128)(2,1)}) %all-gather.2.cloned.1.call-update) | async-done | bytes 9830416 | tf_op jit(solution)/shard_map/all_gather | solution.py:489
  111.6 1.0 slice.68
  113.2 0.6 slice_bitcast_fusion.13.gain_ref
  113.8 1.9 select_reduce_fusion
  115.8 0.8 bitcast_select_fusion.bias_ref
  116.6 129.6 %shard_map.306 = (bf16[2,128,768]{2,1,0:T(8,128)(2,1)}, f32[2,128,768]{2,1,0:T(8,128)}, f32[2,256,192]{2,1,0:T(8,128)}, bf16[2,768,3200]{2,1,0:T(8,128)(2,1)}, f...) custom-call(bf16[128,768]{1,0:T(8,128)(2,1)} %get-tuple-element.110.h_ref, ...), custom_call_target="tpu_custom_call" | custom-call | tf_op jit(solution)/shard_map/pallas_call | solution.py:389
  246.2 1.0 reduce_sum.42
  247.4 0.7 convert_bitcast_fusion
  248.5 0.9 pad_dynamic-update-slice_fusion
  249.4 1.0 copy-done.4
  250.6 0.4 collective-permute-start.1
  251.3 0.5 collective-permute-done.2
  251.9 0.9 copy.89
  252.9 0.8 maximum_bitcast_fusion.2
  253.7 0.9 maximum_bitcast_fusion
  254.6 186.1 %reduce-scatter.2.cloned.1.call-done = bf16[192,3200]{1,0:T(8,128)(2,1)} async-done(((bf16[1536,3200]{1,0:T(8,128)(2,1)}), bf16[192,3200]{1,0:T(8,128)(2,1)}) %reduce-scatter.2.cloned.1.call-update) | async-done | bytes 1228816 | tf_op jit(solution)/shard_map/reduce_scatter | solution.py:537
  440.8 1.4 convert_element_type.44
  442.2 1.2 slice_bitcast_fusion.3
  443.4 1.1 slice_bitcast_fusion
  444.6 0.8 copy.90
  445.4 0.8 copy.91
  446.1 0.7 copy.92
  446.8 0.6 copy.93
  (59 shorter events, 2.9 us)
Async XLA Ops:
  7.2 8.0 %copy-start = (bf16[2,256,768]{2,1,0:T(8,128)(2,1)S(1)}, bf16[2,256,768]{2,1,0:T(8,128)(2,1)}, u32[]{:S(2)}) copy-start(bf16[2,256,768]{2,1,0:T(8,128)(2,1)} %param.20) | copy-start | bytes 2359300
  7.2 7.8 %copy-start.8 = (s32[2,128]{1,0:T(2,128)S(1)}, s32[2,128]{1,0:T(2,128)}, u32[]{:S(2)}) copy-start(s32[2,128]{1,0:T(2,128)} %param.22) | copy-start | bytes 3076
  7.2 7.8 %copy-start.7 = (s32[2,256]{1,0:T(2,128)S(1)}, s32[2,256]{1,0:T(2,128)}, u32[]{:S(2)}) copy-start(s32[2,256]{1,0:T(2,128)} %param.23) | copy-start | bytes 6148
  7.2 7.8 %copy-start.9 = (s32[128]{0:T(128)S(1)}, s32[128]{0:T(128)}, u32[]{:S(2)}) copy-start(s32[128]{0:T(128)} %param.24) | copy-start | bytes 1540
  7.2 104.4 %all-gather.2.cloned.1.call-start = ((), (), s32[]{:S(2)}) async-start(), calls=%async_computation.1 | async-start | bytes 11059200 | tf_op jit(solution)/shard_map/all_gather | solution.py:489
  10.9 5.1 %copy-start.5 = (bf16[2,128,768]{2,1,0:T(8,128)(2,1)S(1)}, bf16[2,128,768]{2,1,0:T(8,128)(2,1)}, u32[]{:S(2)}) copy-start(bf16[2,128,768]{2,1,0:T(8,128)(2,1)} %param.21) | copy-start | bytes 1179652
  10.9 5.0 %copy-start.6 = (bf16[2,128,768]{2,1,0:T(8,128)(2,1)S(1)}, bf16[2,128,768]{2,1,0:T(8,128)(2,1)}, u32[]{:S(2)}) copy-start(bf16[2,128,768]{2,1,0:T(8,128)(2,1)} %param.19) | copy-start | bytes 1179652
  14.8 426.0 %reduce-scatter.2.cloned.1.call-start = ((), (), s32[]{:S(2)}) async-start(), calls=%async_computation.2 | async-start | bytes 11059200 | tf_op jit(solution)/shard_map/reduce_scatter | solution.py:537
  17.0 98.7 %copy-start.1 = (s32[128,128]{1,0:T(8,128)}, s32[128,128]{1,0:T(8,128)S(1)}, u32[]{:S(2)}) copy-start(s32[128,128]{1,0:T(8,128)S(1)} %convert_reduce_fusion.bmap_ref) | copy-start | bytes 196612
  249.3 1.0 copy-start.4
  249.3 1.3 copy-start.2
  249.3 1.7 copy-start.3
  250.4 1.4 collective-permute-start.2
  250.6 3.0 collective-permute-start.1
  251.1 1.7 collective-permute-start
Sparse Core Ops, SparseCore 0:
  14.9 96.6 all-gather.1
  249.5 191.2 reduce-scatter.1

commit v2 on v1

--- a/solution.py
+++ b/solution.py
@@ -269,6 +269,7 @@
     def backward(step, carry):
         l = layers - 1 - step
         base = 3 * layers + 3 * step
+        slot = (l + lax.axis_index("pipe")) % layers
         g3 = g_in[...]
         g = g3.astype(F32)
         gu = gu_s[l]
@@ -282,8 +283,8 @@
             return dot_nt(dgu[part * half : (part + 1) * half], w_ref[l, :, 0 : 2 * ff])
 
         def cover_three():
-            grad_ref[l, :, 0 : 2 * ff] = dot_tn(n_three[l], dgu).astype(BF16)
-            grad_ref[l, :, 2 * ff : 3 * ff] = dot_tn(g3, hid_s[l]).astype(BF16)
+            grad_ref[slot, :, 0 : 2 * ff] = dot_tn(n_three[l], dgu).astype(BF16)
+            grad_ref[slot, :, 2 * ff : 3 * ff] = dot_tn(g3, hid_s[l]).astype(BF16)
 
         dn = all_sum(base, make_three, cover_three)
         back, gain_three = norm_back(r_two[l], gain_ref[l, 2:3], dn)
@@ -321,8 +322,8 @@
                     ).start()
             enc = enc_ref[...]
             block = jnp.concatenate([dot_tn(n_two[l], dcq), dot_tn(enc, dckv)], axis=1)
-            grad_ref[l, :, c_cq:c_co] = block.astype(BF16)
-            grad_ref[l, :, c_co:c_end] = dot_tn(g2b, co).astype(BF16)
+            grad_ref[slot, :, c_cq:c_co] = block.astype(BF16)
+            grad_ref[slot, :, c_co:c_end] = dot_tn(g2b, co).astype(BF16)
 
         dn = all_sum(base + 1, make_two, cover_two)
         back, gain_two = norm_back(r_one[l], gain_ref[l, 1:2], dn)
@@ -344,7 +345,7 @@
             return dot_nt(dqkv[part * half : (part + 1) * half], w_ref[l, :, c_q:c_so])
 
         def cover_one():
-            grad_ref[l, :, c_q:c_cq] = jnp.concatenate(
+            grad_ref[slot, :, c_q:c_cq] = jnp.concatenate(
                 [dot_tn(n_one[l], dqkv), dot_tn(g1b, so)], axis=1
             ).astype(BF16)
             bmap = bmap_ref[...]
@@ -533,10 +534,12 @@
         [gain_grads.transpose(0, 2, 1), table_grads.reshape(layers, D, heads)], axis=2
     )
     tail_grads = jnp.pad(tail_grads, ((0, 0), (0, 0), (0, TAIL - 3 - heads))).astype(BF16)
-    grads = lax.dynamic_update_slice(grads, tail_grads, (0, 0, width - TAIL))
-    summed = lax.psum_scatter(
-        grads.reshape(layers * D, width), ("pipe", "dp"), scatter_dimension=0, tiled=True
-    ).astype(F32)
+    own_tail = lax.dynamic_index_in_dim(tail_grads, mine, 0, keepdims=False)
+    away_tail = lax.dynamic_index_in_dim(tail_grads, 1 - mine, 0, keepdims=False)
+    away = lax.dynamic_update_slice(grads[1], away_tail, (0, width - TAIL))
+    own = lax.dynamic_update_slice(grads[0], own_tail, (0, width - TAIL))
+    merged = (own.astype(F32) + swap(away).astype(F32)).astype(BF16)
+    summed = lax.psum_scatter(merged, "dp", scatter_dimension=0, tiled=True).astype(F32)
     base = 3 * ff
 
     def cut(index):

time: 455 us -> 373 us (0.82)
  waiting for transfers between devices: 280 us -> 180 us
  local copies, waits for them, and re-layouts: 19.9 us -> 30.2 us
  other arithmetic: 9.43 us -> 17.4 us
    reduce_scatter x1, waiting for transfers between devices: 186 us -> 80.6 us  [body(): lax.psum_scatter(merged, 'dp', scatter_dimension=0, tiled=True).astype(F32)]
    squeeze x0 -> x1, local copies, waits for them, and re-layouts: none -> 8.32 us  [body(): own = lax.dynamic_update_slice(grads[0], own_tail, (0, width - TAIL))]
    ppermute x3 -> x4, waiting for transfers between devices: 0.5 us -> 8.13 us  [swap(): return lax.ppermute(value, 'pipe', [(0, 1), (1, 0)])]
    convert_element_type x1 -> x2, other arithmetic: 1.45 us -> 8.7 us  [the longest x1 7.25 us: body(): merged = (own.astype(F32) + swap(away).astype(F32)).astype(BF16)]
  transfers between devices with their start and end apart: 5 -> 6, of which waited for: 3 -> 4; matrix products, arithmetic and copies ran while one was open for 1% -> 2% of each run, Pallas kernels for 0% -> 0%
where the time goes in v2:
time: 373 us
  waiting for transfers between devices  180 us (48%)
  Pallas kernels  130 us (35%)
  local copies, waits for them, and re-layouts  30.2 us (8%)
  other arithmetic  17.4 us (5%)
  between operations  14.3 us (4%)
    pallas_call x1, Pallas kernels, run_main(): pl.pallas_call(functools.partial(main_kernel, dims), out_shape=(jax.Shape...  130 us
    all_gather x1, waiting for transfers between devices, body(): lax.all_gather(packed, ('pipe', 'dp'), axis=0, tiled=True)  91.5 us
    reduce_scatter x1, waiting for transfers between devices, body(): lax.psum_scatter(merged, 'dp', scatter_dimension=0, tiled=True).astype(F32)  80.6 us
    squeeze x1, local copies, waits for them, and re-layouts, body(): own = lax.dynamic_update_slice(grads[0], own_tail, (0, width - TAIL))  8.32 us
    ppermute x4, waiting for transfers between devices, swap(): return lax.ppermute(value, 'pipe', [(0, 1), (1, 0)])  8.13 us
    unnamed x23, local copies, waits for them, and re-layouts  7.96 us
  transfers between devices with their start and end apart: 6, of which 4 were waited for; matrix products, arithmetic and copies ran while one was open for 2% of the time, Pallas kernels for 0%

profile of v2, /device:TPU:0, one launch (start us, length us, event | category | flops | bytes accessed | tf_op | source)
XLA Modules:
  0.0 372.8 jit_solution(7977826638972936233)
XLA Ops:
  7.3 0.9 copy.83
  8.2 0.8 copy.84
  9.0 1.0 copy.81
  10.0 1.0 copy.82
  11.5 3.3 concatenate.7
  15.6 0.7 constant_dynamic-slice_fusion.2
  16.3 0.8 convert_reduce_fusion.1
  17.2 0.8 dynamic-slice_bitcast_fusion.enc_ref
  18.0 0.8 dynamic-slice_bitcast_fusion.2
  19.1 0.7 compare_select_fusion.cmask_ref
  20.2 91.5 %all-gather.2.cloned.1.call-done = bf16[1536,3200]{1,0:T(8,128)(2,1)} async-done(((bf16[192,3200]{1,0:T(8,128)(2,1)}), bf16[1536,3200]{1,0:T(8,128)(2,1)}) %all-gather.2.cloned.1.call-update) | async-done | bytes 9830416 | tf_op jit(solution)/shard_map/all_gather | solution.py:490
  111.7 1.0 slice.76
  113.8 1.9 select_reduce_fusion
  115.8 0.8 bitcast_select_fusion.bias_ref
  116.6 129.8 %shard_map.306 = (bf16[2,128,768]{2,1,0:T(8,128)(2,1)}, f32[2,128,768]{2,1,0:T(8,128)}, f32[2,256,192]{2,1,0:T(8,128)}, bf16[2,768,3200]{2,1,0:T(8,128)(2,1)}, f...) custom-call(bf16[128,768]{1,0:T(8,128)(2,1)} %get-tuple-element.114.h_ref, ...), custom_call_target="tpu_custom_call" | custom-call | tf_op jit(solution)/shard_map/pallas_call | solution.py:390
  246.4 1.0 reduce_sum.42
  247.6 0.7 convert_bitcast_fusion
  248.3 8.3 %slice_bitcast_fusion.1 = (bf16[768,3200]{1,0:T(8,128)(2,1)}, bf16[768,3200]{1,0:T(8,128)(2,1)}) fusion(bf16[2,768,3200]{2,1,0:T(8,128)(2,1)} %get-tuple-element.25), kind=kLoop, calls=%fused_computation.3 | loop fusion | bytes 19660800 | tf_op jit(solution)/shard_map/squeeze | solution.py:540
  256.9 0.7 bitcast_dynamic-update-slice_fusion
  257.8 0.7 bitcast_dynamic-update-slice_fusion.1
  258.5 7.6 %collective-permute-done.3 = bf16[768,3200]{1,0:T(8,128)(2,1)} collective-permute-done((bf16[768,3200]{1,0:T(8,128)(2,1)}, bf16[768,3200]{1,0:T(8,128)(2,1)}, u32[]{:S(2)}, u32[]{:S(2)}) %collective-permute-start.3) | collective-permute-done | bytes 4915232 | tf_op jit(solution)/shard_map/ppermute | solution.py:467
  266.2 7.3 %add_convert_fusion = bf16[768,3200]{1,0:T(8,128)(2,1)} fusion(bf16[768,3200]{1,0:T(8,128)(2,1)} %collective-permute-done.3, bf16[768,3200]{1,0:T(8,128)(2,1)} %bitcast_dynamic-update-slice_fusion.1), kind=kLoop, calls=%fused_computation.1 | loop fusion | flops 9830400 | bytes 14745600 | tf_op jit(solution)/shard_map/convert_element_type | solution.py:541
  273.4 1.0 copy-done.4
  276.0 0.9 copy.94
  276.9 0.8 maximum_bitcast_fusion.2
  277.8 0.9 maximum_bitcast_fusion
  278.7 80.6 %reduce-scatter.2.cloned.1.call-done = bf16[192,3200]{1,0:T(8,128)(2,1)} async-done(((bf16[768,3200]{1,0:T(8,128)(2,1)}), bf16[192,3200]{1,0:T(8,128)(2,1)}) %reduce-scatter.2.cloned.1.call-update) | async-done | bytes 1228816 | tf_op jit(solution)/shard_map/reduce_scatter | solution.py:542
  359.3 1.4 convert_element_type.56
  360.8 1.2 slice_bitcast_fusion.5
  362.0 1.1 slice_bitcast_fusion.2
  363.1 0.8 copy.95
  363.9 0.8 copy.96
  (60 shorter events, 6.8 us)
Async XLA Ops:
  7.2 10.0 %copy-start = (bf16[2,256,768]{2,1,0:T(8,128)(2,1)S(1)}, bf16[2,256,768]{2,1,0:T(8,128)(2,1)}, u32[]{:S(2)}) copy-start(bf16[2,256,768]{2,1,0:T(8,128)(2,1)} %param.20) | copy-start | bytes 2359300
  7.2 10.8 %copy-start.6 = (bf16[2,128,768]{2,1,0:T(8,128)(2,1)S(1)}, bf16[2,128,768]{2,1,0:T(8,128)(2,1)}, u32[]{:S(2)}) copy-start(bf16[2,128,768]{2,1,0:T(8,128)(2,1)} %param.19) | copy-start | bytes 1179652
  7.2 10.8 %copy-start.5 = (bf16[2,128,768]{2,1,0:T(8,128)(2,1)S(1)}, bf16[2,128,768]{2,1,0:T(8,128)(2,1)}, u32[]{:S(2)}) copy-start(bf16[2,128,768]{2,1,0:T(8,128)(2,1)} %param.21) | copy-start | bytes 1179652
  7.2 104.4 %all-gather.2.cloned.1.call-start = ((), (), s32[]{:S(2)}) async-start(), calls=%async_computation.1 | async-start | bytes 11059200 | tf_op jit(solution)/shard_map/all_gather | solution.py:490
  14.8 344.5 %reduce-scatter.2.cloned.1.call-start = ((), (), s32[]{:S(2)}) async-start(), calls=%async_computation.2 | async-start | bytes 6144000 | tf_op jit(solution)/shard_map/reduce_scatter | solution.py:542
  19.0 97.5 %copy-start.1 = (s32[128,128]{1,0:T(8,128)}, s32[128,128]{1,0:T(8,128)S(1)}, u32[]{:S(2)}) copy-start(s32[128,128]{1,0:T(8,128)S(1)} %convert_reduce_fusion.bmap_ref) | copy-start | bytes 196612
  257.6 8.5 %collective-permute-start.3 = (bf16[768,3200]{1,0:T(8,128)(2,1)}, bf16[768,3200]{1,0:T(8,128)(2,1)}, u32[]{:S(2)}, u32[]{:S(2)}) collective-permute-start(bf16[768,3200]{1,0:T(8,128)(2,1)} %bitcast_dynamic-update-slice_fusion), channel_id=1, source_target_pairs={{0,16},{16,0},{1,17},{17,1},{2,18},{18,2},{3,19},{19,3},{4,20},{20... | collective-permute-start | bytes 14745608 | tf_op jit(solution)/shard_map/ppermute | solution.py:467
  273.4 1.0 copy-start.4
  273.4 1.3 copy-start.2
  273.4 1.7 copy-start.3
  274.5 1.4 collective-permute-start.2
  274.7 3.0 collective-permute-start.1
  275.2 1.7 collective-permute-start
Sparse Core Ops, SparseCore 0:
  14.9 96.6 all-gather.1
  273.6 85.7 reduce-scatter.1
